TPU v7x, 32 devices: a whole 2x2x4 slice. The times are simulated.
32 devices in a mesh: batch: 2 (over x), rows: 16 (over z, y, core).
Axes of the slice: x: 2, y: 2, z: 4, core: 2. Of those that a mesh axis runs over, the one named last changes fastest.
Arguments:
- layer_input: bfloat16 [2, 64, 64, 2048], P('batch', 'rows'), may hold values from -6 to 6
- pre_activation: bfloat16 [2, 64, 64, 2048], P('batch', 'rows'), may hold values from -6 to 6
- cotangent: bfloat16 [2, 64, 64, 2048], P('batch', 'rows'), may hold values from -6 to 6
- weight: bfloat16 [64, 64], replicated, may hold values from -0.75 to 0.75
- spectral: bfloat16 [2304, 64, 128], P('rows'), may hold values from -6 to 6
- slab_ids: int32 [2, 32], P('batch'), may hold values from 0 to 2047, as said below
- extents: int32 [2, 32], P('batch'), may hold values from 1 to 2048, as said below
Outputs:
- grad_input: bfloat16 [2, 64, 64, 2048], P('batch', 'rows')
- grad_spectral: float32 [2304, 64, 128], P('rows')
- grad_weight: float32 [64, 64], replicated
Inputs may be any that keep to these rules, and one draw needn't show every extreme that they name: `slab_ids`: within a sample the 32 slab numbers are distinct and include 0 and 2047; slots 2 k to 2 k + 1 are stored on index k of rows. `extents`: A slot's extent counts its slab's live columns from column 0.
All inputs are finite; a program needn't handle non-finite values.
Results may differ from a plain program's by a relative error of at most 0.0085.
Values may be sent and summed in bfloat16 or wider, within the bound.
No kernel may reach another device: no remote copies, remote signals or barrier semaphores. Data moves between devices by JAX's collectives and lax.ppermute only.
A program may use at most 128 MiB of HBM per device.

v0:
```python
import math
import jax
import jax.numpy as jnp
from jax import lax
from jax.sharding import PartitionSpec as P

PA = 48
SLAB = 2
NR = 4096
MODES = 96


def column_table(column_count, freq_count):
    column_index = jnp.arange(column_count, dtype=jnp.int32)
    freq_index = jnp.arange(freq_count, dtype=jnp.int32)
    phase = column_index[:, None] * freq_index[None, :] % column_count
    angle = phase.astype(jnp.float32) * (2.0 * math.pi / column_count)
    return jnp.concatenate([jnp.cos(angle), -jnp.sin(angle)], axis=1).astype(jnp.bfloat16)


def row_table(positions, row_total, freq_count):
    freq_index = jnp.arange(freq_count, dtype=jnp.int32) - freq_count // 2
    phase = jnp.mod(freq_index[:, None] * positions[None, :], row_total)
    angle = phase.astype(jnp.float32) * (2.0 * math.pi / row_total)
    return jnp.concatenate([jnp.cos(angle), jnp.sin(angle)], axis=0).astype(jnp.bfloat16)


def stored_positions(slab_list, slab_rows):
    offsets = jnp.tile(jnp.arange(slab_rows, dtype=jnp.int32), slab_list.shape[0])
    return jnp.repeat(slab_list, slab_rows) * slab_rows + offsets


def gelu_slope(values):
    return (
        0.5 * (1.0 + lax.erf(values * 0.7071067811865476))
        + values * jnp.exp(-0.5 * values * values) * 0.3989422804014327
    )


def row_combine(row_sums, scale):
    upper = row_sums[0]
    lower = row_sums[1]
    real_part = upper[:, :, 0] + lower[:, :, 1]
    imag_part = upper[:, :, 1] - lower[:, :, 0]
    return (jnp.stack([real_part, imag_part], axis=2) * scale).astype(jnp.bfloat16)


def to_blocks(spectra, half_modes):
    chans = spectra.shape[1]
    shaped = spectra.reshape(half_modes, 2, chans, 2, half_modes, 2)
    return shaped.transpose(2, 3, 1, 5, 0, 4).reshape(chans, 2, 2, 2, half_modes * half_modes)


def from_blocks(blocked, half_modes):
    chans = blocked.shape[0]
    shaped = blocked.reshape(chans, 2, 2, 2, half_modes, half_modes)
    return shaped.transpose(4, 2, 0, 1, 5, 3).reshape(2 * half_modes, chans, 2, 2 * half_modes)


def factor_pair(owned, chans):
    input_modes = owned[:chans]
    grad_out = owned[chans:]
    factor_left = input_modes.transpose(4, 0, 1, 2, 3).reshape(owned.shape[4], chans, 8)
    real_out = grad_out[:, 0]
    imag_out = grad_out[:, 1]
    first_half = jnp.stack([real_out, imag_out], axis=1)
    second_half = jnp.stack([imag_out, -real_out], axis=1)
    stacked = jnp.concatenate([first_half, second_half], axis=0)
    factor_right = stacked.transpose(4, 0, 1, 2, 3).reshape(owned.shape[4], 2 * chans, 8)
    return (factor_left, factor_right)


def modes_to_channels(grad_modes):
    blocks = grad_modes.shape[0]
    chans = grad_modes.shape[1]
    return grad_modes.reshape(blocks, chans, 2, 2, 2).transpose(1, 2, 3, 4, 0)


def row_adjoint(rowtab, grad_grid, scale):
    real_part = grad_grid[:, :, 0]
    imag_part = grad_grid[:, :, 1]
    upper = jnp.stack([real_part, imag_part], axis=2)
    lower = jnp.stack([-imag_part, real_part], axis=2)
    joined = jnp.concatenate([upper, lower], axis=0)
    summed = jnp.dot(
        rowtab.T, joined.reshape(joined.shape[0], -1), preferred_element_type=jnp.float32
    )
    return (summed * scale).astype(jnp.bfloat16)


def shards(layer_input, pre_activation, cotangent, weight, spectral, slab_ids, extents):
    batch_devices = lax.axis_size("batch")
    local_rows = layer_input.shape[1]
    channels = layer_input.shape[2]
    column_count = layer_input.shape[3]
    slab_list = slab_ids[0]
    active = slab_list.shape[0]
    slots = local_rows // SLAB
    scale = 1.0 / math.sqrt(NR * column_count)
    position = lax.axis_index("rows")
    own_extents = lax.dynamic_slice_in_dim(extents[0], position * slots, slots)
    column_index = jnp.arange(column_count, dtype=jnp.int32)
    alive = column_index[None, :] < jnp.repeat(own_extents, SLAB)[:, None]
    mask_half = alive.astype(jnp.bfloat16)
    mask_full = alive.astype(jnp.float32)
    masked_in = layer_input[0] * mask_half[:, None, :]
    grad_pre = (
        cotangent[0].astype(jnp.float32)
        * mask_full[:, None, :]
        * gelu_slope(pre_activation[0].astype(jnp.float32))
    ).astype(jnp.bfloat16)
    coltab = column_table(column_count, MODES)
    stacked = jnp.concatenate([masked_in, grad_pre], axis=1)
    colspec = jnp.dot(stacked.reshape(-1, column_count), coltab, preferred_element_type=jnp.float32)
    colspec = colspec.reshape(local_rows, 2 * channels, 2 * MODES).astype(jnp.bfloat16)
    gathered_rows = lax.all_to_all(colspec, "rows", split_axis=1, concat_axis=0, tiled=True)
    all_rows = gathered_rows.shape[0]
    owned_channels = gathered_rows.shape[1]
    rowtab = row_table(stored_positions(slab_list, SLAB), NR, MODES)
    row_sums = jnp.dot(
        rowtab, gathered_rows.reshape(all_rows, -1), preferred_element_type=jnp.float32
    )
    spectra = row_combine(row_sums.reshape(2, MODES, owned_channels, 2, MODES), scale)
    owned = lax.all_to_all(to_blocks(spectra, PA), "rows", split_axis=4, concat_axis=0, tiled=True)
    factor_left, factor_right = factor_pair(owned, channels)
    grad_modes = jnp.einsum(
        "bix,bxk->bik", spectral, factor_right, preferred_element_type=jnp.float32
    ).astype(jnp.bfloat16)
    own_grad = jnp.einsum(
        "bik,bxk->bix", factor_left, factor_right, preferred_element_type=jnp.float32
    )
    grad_spectral = lax.psum(own_grad, "batch")
    returned = lax.all_to_all(
        modes_to_channels(grad_modes), "rows", split_axis=0, concat_axis=4, tiled=True
    )
    rowback = row_adjoint(rowtab, from_blocks(returned, PA), scale)
    rowback = rowback.reshape(all_rows, -1, 2 * MODES)
    local_back = lax.all_to_all(rowback, "rows", split_axis=0, concat_axis=1, tiled=True)
    spatial = jnp.dot(
        local_back.reshape(-1, 2 * MODES), coltab.T, preferred_element_type=jnp.float32
    )
    spatial = spatial.reshape(local_rows, channels, column_count)
    row_weight = jnp.broadcast_to(weight, (local_rows, channels, channels))
    direct = jnp.einsum("rio,roc->ric", row_weight, grad_pre, preferred_element_type=jnp.float32)
    grad_input = ((spatial + direct) * mask_full[:, None, :]).astype(jnp.bfloat16)[None]
    row_partial = jnp.einsum(
        "ric,roc->rio", masked_in, grad_pre, preferred_element_type=jnp.float32
    )
    local_weight = jnp.sum(row_partial, axis=0)
    grad_weight = lax.psum(local_weight, ("batch", "rows"))
    grad_weight = grad_weight * (1.0 / math.sqrt(batch_devices * active * SLAB * column_count))
    return (grad_input, grad_spectral, grad_weight)


def solution(mesh):
    return jax.shard_map(
        shards,
        mesh=mesh,
        in_specs=(
            P("batch", "rows", None, None),
            P("batch", "rows", None, None),
            P("batch", "rows", None, None),
            P(),
            P("rows", None, None),
            P("batch", None),
            P("batch", None),
        ),
        out_specs=(P("batch", "rows", None, None), P("rows", None, None), P()),
        check_vma=False,
    )
```

profile of v0, /device:TPU:0, one launch (start us, length us, event | category | flops | bytes accessed | tf_op | source)
XLA Modules:
  0.0 304.3 jit_solution(13098841507869636662)
XLA Ops:
  7.2 3.9 %negate_convert_fusion = (bf16[2048,96]{0,1:T(8,128)(2,1)}, bf16[2048,96]{0,1:T(8,128)(2,1)}) fusion(), kind=kLoop, calls=%fused_computation.40 | loop fusion | flops 3342336 | bytes 786432 | tf_op jit(solution)/shard_map/convert.3
  15.1 1.6 fusion.17
  16.6 1.8 copy.52
  18.4 7.5 %all-to-all-start = ((bf16[4,128,192]{2,0,1:T(4,128)(2,1)}), bf16[4,128,192]{2,0,1:T(4,128)(2,1)}, u32[]{:S(2)}, u32[]{:S(2)}) async-start(bf16[4,128,192]{2,0,1:T(4,128)(2,1)} %copy.52), calls=%async_computation | async-start | bytes 524288 | tf_op jit(solution)/shard_map/all_to_all | solution.py:116
  26.6 9.3 %all-to-all-done = bf16[4,128,192]{2,0,1:T(4,128)(2,1)} async-done(((bf16[4,128,192]{2,0,1:T(4,128)(2,1)}), bf16[4,128,192]{2,0,1:T(4,128)(2,1)}, u32[]{:S(2)}, u32[]{:S(2)}) %all-to-all-start) | async-done | bytes 196640 | tf_op jit(solution)/shard_map/all_to_all | solution.py:116
  37.7 1.9 reshape.119
  41.9 3.0 squeeze.7
  44.8 3.1 %fusion.45 = (f32[96,8,1,96]{3,2,1,0:T(1,128)}, f32[96,8,1,96]{3,2,1,0:T(1,128)}) fusion(f32[96,8,2,96]{3,2,1,0:T(2,128)} %squeeze.7), kind=kLoop, calls=%fused_computation.82 | loop fusion | bytes 1179648 | tf_op jit(solution)/shard_map/slice | solution.py:43
  47.9 4.2 %copy.79 = f32[96,8,1,96]{1,3,0,2:T(8,128)} copy(f32[96,8,1,96]{3,2,1,0:T(1,128)} %get-tuple-element.10) | data formatting | bytes 589824
  52.1 3.0 squeeze.8
  55.1 2.9 fusion.44
  58.0 4.2 %copy.80 = f32[96,8,1,96]{1,3,0,2:T(8,128)} copy(f32[96,8,1,96]{3,2,1,0:T(1,128)} %get-tuple-element.8) | data formatting | bytes 589824
  62.2 6.9 %sub.9 = f32[96,8,1,96]{1,3,0,2:T(8,128)} subtract(f32[96,8,1,96]{1,3,0,2:T(8,128)} %copy.79, f32[96,8,1,96]{1,3,0,2:T(8,128)} %copy.80) | non-fusion elementwise | flops 73728 | bytes 884736 | tf_op jit(solution)/shard_map/sub | solution.py:44
  69.1 6.2 %copy.60 = f32[48,2,8,1,48,2]{4,2,5,3,1,0:T(8,128)} copy(f32[48,2,8,1,48,2]{2,5,4,1,0,3:T(2,128)} %bitcast.84) | data formatting | bytes 589824 | tf_op jit(solution)/shard_map/stack | solution.py:45
  75.3 4.2 %copy.77 = f32[96,8,1,96]{1,3,0,2:T(8,128)} copy(f32[96,8,1,96]{3,2,1,0:T(1,128)} %get-tuple-element.9) | data formatting | bytes 589824
  79.5 4.2 %copy.78 = f32[96,8,1,96]{1,3,0,2:T(8,128)} copy(f32[96,8,1,96]{3,2,1,0:T(1,128)} %get-tuple-element.7) | data formatting | bytes 589824
  83.7 6.9 %add.60 = f32[96,8,1,96]{1,3,0,2:T(8,128)} add(f32[96,8,1,96]{1,3,0,2:T(8,128)} %copy.77, f32[96,8,1,96]{1,3,0,2:T(8,128)} %copy.78) | non-fusion elementwise | flops 73728 | bytes 884736 | tf_op jit(solution)/shard_map/add | solution.py:43
  90.6 6.2 %copy.59 = f32[48,2,8,1,48,2]{4,2,5,3,1,0:T(8,128)} copy(f32[48,2,8,1,48,2]{2,5,4,1,0,3:T(2,128)} %bitcast.85) | data formatting | bytes 589824 | tf_op jit(solution)/shard_map/stack | solution.py:45
  96.8 2.5 fusion.24
  99.3 9.3 %copy.74 = bf16[8,2,2,2,48,48]{0,3,2,1,5,4:T(2,128)(2,1)} copy(bf16[8,2,2,2,48,48]{5,0,3,1,2,4:T(8,128)(2,1)} %fusion.24) | data formatting | bytes 589824 | tf_op jit(solution)/shard_map/reshape | solution.py:51
  108.6 7.0 %reshape.131 = bf16[16,2,4608]{2,1,0:T(2,128)(2,1)} reshape(bf16[2304,2,2,2,8]{4,3,2,1,0:T(2,128)(2,1)} %bitcast.87) | data formatting | bytes 589824
  115.6 14.7 %all_to_all.60 = bf16[16,2,4608]{2,1,0:T(2,128)(2,1)} all-to-all(bf16[16,2,4608]{2,1,0:T(2,128)(2,1)} %reshape.131), channel_id=1, replica_groups=mesh['batch'=2,'rows'=16] {'rows'}, dimensions={0} | all-to-all | bytes 589824 | tf_op jit(solution)/shard_map/all_to_all | solution.py:124
  130.3 7.4 %reshape.132 = bf16[2304,2,2,2,8]{4,3,2,1,0:T(2,128)(2,1)} reshape(bf16[16,2,4608]{2,1,0:T(2,128)(2,1)} %all_to_all.60) | data formatting | bytes 589824
  137.7 12.1 %copy.75 = bf16[8,2,2,2,16,144]{5,4,0,3,2,1:T(8,128)(2,1)} copy(bf16[8,2,2,2,16,144]{0,3,2,1,5,4:T(2,128)(2,1)} %bitcast.88) | data formatting | bytes 589824 | tf_op jit(solution)/shard_map/all_to_all | solution.py:124
  149.8 1.8 fusion.46
  152.5 1.9 copy.65
  154.5 1.7 copy.85
  156.2 1.9 copy.73
  158.1 4.0 %fusion.48 = f32[144,64,128]{2,1,0:T(8,128)} fusion(bf16[144,64,8]{1,2,0:T(8,128)(2,1)} %bitcast.97, bf16[144,128,8]{1,2,0:T(8,128)(2,1)} %bitcast.91), kind=kOutput, calls=%fused_computation.85 | convolution fusion | flops 18874368 | bytes 5160960 | tf_op jit(solution)/shard_map/bik,bxk->bix/dot_general | solution.py:129
  162.1 3.0 convolution_convert_fusion
  165.1 2.0 copy.66
  167.1 4.2 %all-to-all-start.2 = ((bf16[64,2,2,2,144]{4,3,2,1,0:T(2,128)(2,1)}), bf16[64,2,2,2,144]{4,3,2,1,0:T(2,128)(2,1)}, u32[]{:S(2)}, u32[]{:S(2)}) async-start(bf16[64,2,2,2,144]{4,3,2,1,0:T(2,128)(2,1)} %bitcast.98), calls=%async_computation.2 | async-start | bytes 524288 | tf_op jit(solution)/shard_map/all_to_all | solution.py:133
  171.3 1.6 convolution_bitcast_fusion.1
  173.0 42.4 %psum.15 = f32[64,64]{1,0:T(8,128)} all-reduce(f32[64,64]{1,0:T(8,128)S(1)} %convolution_bitcast_fusion.1), channel_id=1, replica_groups=mesh['batch'=2,'rows'=16] {'batch','rows'}, use_global_device_ids=true, to_apply=%region_1.2 | all-reduce | flops 4096 | bytes 32768 | tf_op jit(solution)/shard_map/psum | solution.py:150
  215.4 1.8 copy.67
  217.2 2.1 reshape.123
  219.3 13.9 %copy.69 = bf16[48,2,4,2,48,2]{2,5,4,3,1,0:T(2,128)(2,1)} copy(bf16[48,2,4,2,48,2]{4,0,5,1,3,2:T(8,128)(2,1)} %bitcast.89) | data formatting | bytes 294912 | tf_op jit(solution)/shard_map/transpose | solution.py:57
  233.2 8.4 %copy.68 = bf16[48,2,4,2,48,2]{5,4,3,2,1,0:T(8,128)(2,1)} copy(bf16[48,2,4,2,48,2]{4,0,5,1,3,2:T(8,128)(2,1)} %bitcast.90) | data formatting | bytes 294912 | tf_op jit(solution)/shard_map/transpose | solution.py:57
  241.7 2.9 slice_negate_fusion
  244.5 3.1 %pad_maximum_fusion = bf16[96,4,2,96]{1,3,2,0:T(8,128)(2,1)} fusion(bf16[96,4,1,96]{1,3,2,0:T(8,128)(2,1)S(1)} %get-tuple-element.4, bf16[96,4,1,96]{1,3,2,0:T(8,128)(2,1)S(1)} %get-tuple-element.3), kind=kLoop, calls=%fused_computation | loop fusion | flops 73728 | bytes 294912 | tf_op jit(solution)/shard_map/stack | solution.py:83
  247.6 4.9 %copy.70 = bf16[96,4,2,96]{3,2,1,0:T(2,128)(2,1)} copy(bf16[96,4,2,96]{1,3,2,0:T(8,128)(2,1)} %pad_maximum_fusion) | data formatting | bytes 294912 | tf_op jit(solution)/shard_map/stack | solution.py:83
  253.7 17.1 %concatenate.27 = bf16[96,768]{1,0:T(8,128)(2,1)} reshape(bf16[48,2,4,2,48,2]{5,4,3,2,1,0:T(8,128)(2,1)} %copy.68) | data formatting | bytes 294912 | tf_op jit(solution)/shard_map/concatenate | solution.py:84
  270.7 1.8 fusion.20
  272.5 1.7 reshape.125
  274.2 5.3 %all-to-all-start.3 = ((bf16[64,4,192]{2,1,0:T(4,128)(2,1)}), bf16[64,4,192]{2,1,0:T(4,128)(2,1)S(1)}, u32[]{:S(2)}, u32[]{:S(2)}) async-start(bf16[64,4,192]{2,1,0:T(4,128)(2,1)} %reshape.125), calls=%async_computation.3 | async-start | bytes 262144 | tf_op jit(solution)/shard_map/all_to_all | solution.py:138
  281.0 6.5 %all-to-all-done.3 = bf16[64,4,192]{2,1,0:T(4,128)(2,1)S(1)} async-done(((bf16[64,4,192]{2,1,0:T(4,128)(2,1)}), bf16[64,4,192]{2,1,0:T(4,128)(2,1)S(1)}, u32[]{:S(2)}, u32[]{:S(2)}) %all-to-all-start.3) | async-done | bytes 98336 | tf_op jit(solution)/shard_map/all_to_all | solution.py:138
  289.2 1.5 fusion.28
  292.2 5.2 %copy.90 = f32[144,64,128]{2,1,0:T(8,128)} copy(f32[144,64,128]{2,1,0:T(8,128)} %all-reduce.2.cloned.1.call-done) | data formatting | bytes 9437184
  (51 shorter events, 15.2 us)
Async XLA Ops:
  7.2 154.9 %copy-start = (bf16[144,64,128]{2,1,0:T(8,128)(2,1)S(1)}, bf16[144,64,128]{2,1,0:T(8,128)(2,1)}, u32[]{:S(2)}) copy-start(bf16[144,64,128]{2,1,0:T(8,128)(2,1)} %param.11) | copy-start | bytes 7077892
  11.9 1.6 copy-start.4
  11.9 1.9 copy-start.5
  12.0 2.9 copy-start.6
  13.5 1.4 copy-start.1
  13.5 1.4 copy-start.2
  13.5 1.6 copy-start.3
  15.1 11.1 %copy-start.11 = (s32[1,32]{1,0:T(1,128)S(1)}, s32[1,32]{1,0:T(1,128)}, u32[]{:S(2)}) copy-start(s32[1,32]{1,0:T(1,128)} %param.12) | copy-start | bytes 388
  18.4 17.5 %all-to-all-start = ((bf16[4,128,192]{2,0,1:T(4,128)(2,1)}), bf16[4,128,192]{2,0,1:T(4,128)(2,1)}, u32[]{:S(2)}, u32[]{:S(2)}) async-start(bf16[4,128,192]{2,0,1:T(4,128)(2,1)} %copy.52), calls=%async_computation | async-start | bytes 524288 | tf_op jit(solution)/shard_map/all_to_all | solution.py:116
  25.9 266.3 %all-reduce.2.cloned.1.call-start = ((), (), s32[]{:S(2)}) async-start(), calls=%async_computation.4 | async-start | bytes 9437184 | tf_op jit(solution)/shard_map/psum | solution.py:132
  26.6 15.2 %copy-start.8 = (bf16[96,64]{1,0:T(8,128)(2,1)}, bf16[96,64]{1,0:T(8,128)(2,1)S(1)}, u32[]{:S(2)}) copy-start(bf16[96,64]{1,0:T(8,128)(2,1)S(1)} %get-tuple-element.15) | copy-start | bytes 36868
  26.6 15.2 %copy-start.9 = (bf16[96,64]{1,0:T(8,128)(2,1)}, bf16[96,64]{1,0:T(8,128)(2,1)S(1)}, u32[]{:S(2)}) copy-start(bf16[96,64]{1,0:T(8,128)(2,1)S(1)} %get-tuple-element.16) | copy-start | bytes 36868
  167.1 48.3 %all-to-all-start.2 = ((bf16[64,2,2,2,144]{4,3,2,1,0:T(2,128)(2,1)}), bf16[64,2,2,2,144]{4,3,2,1,0:T(2,128)(2,1)}, u32[]{:S(2)}, u32[]{:S(2)}) async-start(bf16[64,2,2,2,144]{4,3,2,1,0:T(2,128)(2,1)} %bitcast.98), calls=%async_computation.2 | async-start | bytes 524288 | tf_op jit(solution)/shard_map/all_to_all | solution.py:133
  272.5 18.2 %copy-start.10 = (bf16[64,64]{1,0:T(8,128)(2,1)S(1)}, bf16[64,64]{1,0:T(8,128)(2,1)}, u32[]{:S(2)}) copy-start(bf16[64,64]{1,0:T(8,128)(2,1)} %param.10) | copy-start | bytes 24580
  274.2 13.2 %all-to-all-start.3 = ((bf16[64,4,192]{2,1,0:T(4,128)(2,1)}), bf16[64,4,192]{2,1,0:T(4,128)(2,1)S(1)}, u32[]{:S(2)}, u32[]{:S(2)}) async-start(bf16[64,4,192]{2,1,0:T(4,128)(2,1)} %reshape.125), calls=%async_computation.3 | async-start | bytes 262144 | tf_op jit(solution)/shard_map/all_to_all | solution.py:138
  289.2 1.6 copy-start.7
Sparse Core Ops, SparseCore 0:
  162.2 119.0 all-reduce.1
where the time goes:
time: 309 us; the launch traced here: 304 us
  local copies, waits for them, and re-layouts  152 us (49%)
  blocking collectives  57.2 us (19%)
  other arithmetic  31.5 us (10%)
  starting transfers between devices  17.2 us (6%)
  matrix products  16.2 us (5%)
  waiting for transfers between devices  15.9 us (5%)
  between operations  14.3 us (5%)
    psum x1, blocking collectives, shards(): grad_weight = lax.psum(local_weight, ('batch', 'rows'))  42.4 us
    unnamed x31, local copies, waits for them, and re-layouts  36.7 us
    transpose x2, local copies, waits for them, and re-layouts, from_blocks(): shaped.transpose(4, 2, 0, 1, 5, 3)  22.3 us
    concatenate x2, local copies, waits for them, and re-layouts, row_adjoint(): joined = jnp.concatenate([upper, lower], axis=0)  18.2 us
    all_to_all x1, blocking collectives, shards(): lax.all_to_all(to_blocks(spectra, PA), 'rows', split_axis=4, concat_axis=...  14.7 us
    another operation x2, local copies, waits for them, and re-layouts, row_combine(): jnp.stack([real_part, imag_part], axis=2) * scale  12.3 us
    all_to_all x1, local copies, waits for them, and re-layouts, shards(): lax.all_to_all(to_blocks(spectra, PA), 'rows', split_axis=4, concat_axis=...  12.1 us
    all_to_all x1, waiting for transfers between devices, shards(): lax.all_to_all(colspec, 'rows', split_axis=1, concat_axis=0, tiled=True)  9.32 us
  transfers between devices with their start and end apart: 4, of which 2 were waited for; matrix products, arithmetic and copies ran while one was open for 24% of the time, Pallas kernels for 0%

commit v1 on v0

--- a/solution.py
+++ b/solution.py
@@ -121,7 +121,15 @@
         rowtab, gathered_rows.reshape(all_rows, -1), preferred_element_type=jnp.float32
     )
     spectra = row_combine(row_sums.reshape(2, MODES, owned_channels, 2, MODES), scale)
-    owned = lax.all_to_all(to_blocks(spectra, PA), "rows", split_axis=4, concat_axis=0, tiled=True)
+    owned = jnp.concatenate(
+        lax.all_to_all(
+            jnp.stack(jnp.split(to_blocks(spectra, PA), lax.axis_size("rows"), axis=4), 0),
+            "rows",
+            0,
+            0,
+        ),
+        0,
+    )
     factor_left, factor_right = factor_pair(owned, channels)
     grad_modes = jnp.einsum(
         "bix,bxk->bik", spectral, factor_right, preferred_element_type=jnp.float32

time: 309 us -> 291 us (0.942)
  local copies, waits for them, and re-layouts: 152 us -> 133 us
    all_to_all x1 -> x0, local copies, waits for them, and re-layouts: 12.1 us -> none  [shards(): lax.all_to_all(to_blocks(spectra, PA), 'rows', split_axis=4, concat_axis=...]
    reshape x1, local copies, waits for them, and re-layouts: 9.32 us -> 2.61 us  [to_blocks(): shaped.transpose(2, 3, 1, 5, 0, 4)]
    unnamed x31 -> x44, local copies, waits for them, and re-layouts: 36.7 us -> 35.3 us
  transfers between devices with their start and end apart: 4 -> 4, of which waited for: 2 -> 2; matrix products, arithmetic and copies ran while one was open for 24% -> 25% of each run, Pallas kernels for 0% -> 0%
where the time goes in v1:
time: 291 us; the launch traced here: 286 us
  local copies, waits for them, and re-layouts  133 us (46%)
  blocking collectives  59.3 us (20%)
  other arithmetic  30.6 us (11%)
  starting transfers between devices  17.5 us (6%)
  matrix products  16.2 us (6%)
  waiting for transfers between devices  15.9 us (5%)
  between operations  14.3 us (5%)
    psum x1, blocking collectives, shards(): grad_weight = lax.psum(local_weight, ('batch', 'rows'))  42.3 us
    unnamed x44, local copies, waits for them, and re-layouts  35.3 us
    transpose x2, local copies, waits for them, and re-layouts, from_blocks(): shaped.transpose(4, 2, 0, 1, 5, 3)  22.3 us
    concatenate x2, local copies, waits for them, and re-layouts, row_adjoint(): joined = jnp.concatenate([upper, lower], axis=0)  18.2 us
    all_to_all x1, blocking collectives, shards(): lax.all_to_all(jnp.stack(jnp.split(to_blocks(spectra, PA), lax.axis_size(...  16.9 us
    another operation x2, local copies, waits for them, and re-layouts, row_combine(): jnp.stack([real_part, imag_part], axis=2) * scale  12.3 us
    all_to_all x1, waiting for transfers between devices, shards(): lax.all_to_all(colspec, 'rows', split_axis=1, concat_axis=0, tiled=True)  9.32 us
    all_to_all x1, starting transfers between devices, shards(): lax.all_to_all(colspec, 'rows', split_axis=1, concat_axis=0, tiled=True)  7.46 us
  transfers between devices with their start and end apart: 4, of which 2 were waited for; matrix products, arithmetic and copies ran while one was open for 25% of the time, Pallas kernels for 0%

profile of v1, /device:TPU:0, one launch (start us, length us, event | category | flops | bytes accessed | tf_op | source)
XLA Modules:
  0.0 286.5 jit_solution(14743403533956134839)
XLA Ops:
  7.2 3.9 %negate_convert_fusion = (bf16[2048,96]{0,1:T(8,128)(2,1)}, bf16[2048,96]{0,1:T(8,128)(2,1)}) fusion(), kind=kLoop, calls=%fused_computation.40 | loop fusion | flops 3342336 | bytes 786432 | tf_op jit(solution)/shard_map/convert.3
  12.0 1.4 bitcast_multiply_fusion
  15.1 1.6 fusion.17
  16.6 1.8 copy.65
  18.4 7.5 %all-to-all-start = ((bf16[4,128,192]{2,0,1:T(4,128)(2,1)}), bf16[4,128,192]{2,0,1:T(4,128)(2,1)}, u32[]{:S(2)}, u32[]{:S(2)}) async-start(bf16[4,128,192]{2,0,1:T(4,128)(2,1)} %copy.65), calls=%async_computation | async-start | bytes 524288 | tf_op jit(solution)/shard_map/all_to_all | solution.py:116
  26.6 9.3 %all-to-all-done = bf16[4,128,192]{2,0,1:T(4,128)(2,1)} async-done(((bf16[4,128,192]{2,0,1:T(4,128)(2,1)}), bf16[4,128,192]{2,0,1:T(4,128)(2,1)}, u32[]{:S(2)}, u32[]{:S(2)}) %all-to-all-start) | async-done | bytes 196640 | tf_op jit(solution)/shard_map/all_to_all | solution.py:116
  37.7 1.9 reshape.120
  41.9 3.0 %squeeze.7 = f32[96,8,2,96]{3,2,1,0:T(2,128)} reshape(f32[96,1536]{1,0:T(8,128)} %get-tuple-element.6) | data formatting | bytes 1179648 | tf_op jit(solution)/shard_map/squeeze | solution.py:41
  44.8 3.1 %fusion.45 = (f32[96,8,1,96]{3,2,1,0:T(1,128)}, f32[96,8,1,96]{3,2,1,0:T(1,128)}) fusion(f32[96,8,2,96]{3,2,1,0:T(2,128)} %squeeze.7), kind=kLoop, calls=%fused_computation.114 | loop fusion | bytes 1179648 | tf_op jit(solution)/shard_map/slice | solution.py:43
  47.9 4.2 %copy.87 = f32[96,8,1,96]{1,3,0,2:T(8,128)} copy(f32[96,8,1,96]{3,2,1,0:T(1,128)} %get-tuple-element.10) | data formatting | bytes 589824
  52.1 3.0 %squeeze.8 = f32[96,8,2,96]{3,2,1,0:T(2,128)} reshape(f32[96,1536]{1,0:T(8,128)} %get-tuple-element.5) | data formatting | bytes 1179648 | tf_op jit(solution)/shard_map/squeeze | solution.py:42
  55.1 2.9 %fusion.44 = (f32[96,8,1,96]{3,2,1,0:T(1,128)}, f32[96,8,1,96]{3,2,1,0:T(1,128)}) fusion(f32[96,8,2,96]{3,2,1,0:T(2,128)} %squeeze.8), kind=kLoop, calls=%fused_computation.113 | loop fusion | bytes 1179648 | tf_op jit(solution)/shard_map/slice | solution.py:43
  58.0 4.2 %copy.88 = f32[96,8,1,96]{1,3,0,2:T(8,128)} copy(f32[96,8,1,96]{3,2,1,0:T(1,128)} %get-tuple-element.8) | data formatting | bytes 589824
  62.2 6.9 %sub.9 = f32[96,8,1,96]{1,3,0,2:T(8,128)} subtract(f32[96,8,1,96]{1,3,0,2:T(8,128)} %copy.87, f32[96,8,1,96]{1,3,0,2:T(8,128)} %copy.88) | non-fusion elementwise | flops 73728 | bytes 884736 | tf_op jit(solution)/shard_map/sub | solution.py:44
  69.1 6.2 %copy.73 = f32[48,2,8,1,48,2]{4,2,5,3,1,0:T(8,128)} copy(f32[48,2,8,1,48,2]{2,5,4,1,0,3:T(2,128)} %bitcast.147) | data formatting | bytes 589824 | tf_op jit(solution)/shard_map/stack | solution.py:45
  75.3 4.2 %copy.85 = f32[96,8,1,96]{1,3,0,2:T(8,128)} copy(f32[96,8,1,96]{3,2,1,0:T(1,128)} %get-tuple-element.9) | data formatting | bytes 589824
  79.5 4.2 %copy.86 = f32[96,8,1,96]{1,3,0,2:T(8,128)} copy(f32[96,8,1,96]{3,2,1,0:T(1,128)} %get-tuple-element.7) | data formatting | bytes 589824
  83.7 6.9 %add.60 = f32[96,8,1,96]{1,3,0,2:T(8,128)} add(f32[96,8,1,96]{1,3,0,2:T(8,128)} %copy.85, f32[96,8,1,96]{1,3,0,2:T(8,128)} %copy.86) | non-fusion elementwise | flops 73728 | bytes 884736 | tf_op jit(solution)/shard_map/add | solution.py:43
  90.6 6.2 %copy.72 = f32[48,2,8,1,48,2]{4,2,5,3,1,0:T(8,128)} copy(f32[48,2,8,1,48,2]{2,5,4,1,0,3:T(2,128)} %bitcast.148) | data formatting | bytes 589824 | tf_op jit(solution)/shard_map/stack | solution.py:45
  96.8 1.6 fusion.24
  98.4 1.4 copy.74
  99.8 2.6 reshape.121
  116.2 16.9 %all_to_all.50 = bf16[16,8,2,2,2,144]{5,1,4,3,2,0:T(8,128)(2,1)S(1)} all-to-all(bf16[16,8,2,2,2,144]{5,1,4,3,2,0:T(8,128)(2,1)S(1)} %constant_dynamic-update-slice_fusion), channel_id=1, replica_groups=mesh['batch'=2,'rows'=16] {'rows'}, dimensions={0} | all-to-all | bytes 589824 | tf_op jit(solution)/shard_map/all_to_all | solution.py:125
  134.8 1.9 copy.76
  136.7 1.7 copy.93
  138.4 1.9 copy.84
  140.2 4.0 %fusion.48 = f32[144,64,128]{2,1,0:T(8,128)} fusion(bf16[144,64,8]{1,2,0:T(8,128)(2,1)} %bitcast.157, bf16[144,128,8]{1,2,0:T(8,128)(2,1)} %bitcast.152), kind=kOutput, calls=%fused_computation.117 | convolution fusion | flops 18874368 | bytes 5160960 | tf_op jit(solution)/shard_map/bik,bxk->bix/dot_general | solution.py:137
  144.3 3.0 %convolution_convert_fusion = bf16[144,8,64]{2,1,0:T(8,128)(2,1)} fusion(bf16[144,128,8]{1,2,0:T(8,128)(2,1)} %bitcast.153, bf16[144,64,128]{2,1,0:T(8,128)(2,1)S(1)} %copy-done), kind=kOutput, calls=%fused_computation.26 | convolution fusion | flops 18948096 | bytes 2801664 | tf_op jit(solution)/shard_map/bix,bxk->bik/dot_general | solution.py:134
  147.3 2.0 copy.77
  149.3 4.4 %all-to-all-start.2 = ((bf16[64,2,2,2,144]{4,3,2,1,0:T(2,128)(2,1)}), bf16[64,2,2,2,144]{4,3,2,1,0:T(2,128)(2,1)}, u32[]{:S(2)}, u32[]{:S(2)}) async-start(bf16[64,2,2,2,144]{4,3,2,1,0:T(2,128)(2,1)} %bitcast.158), calls=%async_computation.2 | async-start | bytes 524288 | tf_op jit(solution)/shard_map/all_to_all | solution.py:141
  153.7 1.6 convolution_bitcast_fusion.1
  155.4 42.3 %psum.15 = f32[64,64]{1,0:T(8,128)} all-reduce(f32[64,64]{1,0:T(8,128)S(1)} %convolution_bitcast_fusion.1), channel_id=1, replica_groups=mesh['batch'=2,'rows'=16] {'batch','rows'}, use_global_device_ids=true, to_apply=%region_1.2 | all-reduce | flops 4096 | bytes 32768 | tf_op jit(solution)/shard_map/psum | solution.py:158
  197.7 1.8 copy.78
  199.5 2.1 reshape.124
  201.6 13.9 %copy.80 = bf16[48,2,4,2,48,2]{2,5,4,3,1,0:T(2,128)(2,1)} copy(bf16[48,2,4,2,48,2]{4,0,5,1,3,2:T(8,128)(2,1)} %bitcast.150) | data formatting | bytes 294912 | tf_op jit(solution)/shard_map/transpose | solution.py:57
  215.5 8.4 %copy.79 = bf16[48,2,4,2,48,2]{5,4,3,2,1,0:T(8,128)(2,1)} copy(bf16[48,2,4,2,48,2]{4,0,5,1,3,2:T(8,128)(2,1)} %bitcast.151) | data formatting | bytes 294912 | tf_op jit(solution)/shard_map/transpose | solution.py:57
  223.9 2.9 %slice_negate_fusion = (bf16[96,4,1,96]{1,3,2,0:T(8,128)(2,1)S(1)}, bf16[96,4,1,96]{1,3,2,0:T(8,128)(2,1)S(1)}) fusion(bf16[96,4,2,96]{1,3,2,0:T(8,128)(2,1)} %bitcast.149), kind=kLoop, calls=%fused_computation.10 | loop fusion | flops 36864 | bytes 294912 | tf_op jit(solution)/shard_map/neg | solution.py:83
  226.8 3.1 %pad_maximum_fusion = bf16[96,4,2,96]{1,3,2,0:T(8,128)(2,1)} fusion(bf16[96,4,1,96]{1,3,2,0:T(8,128)(2,1)S(1)} %get-tuple-element.4, bf16[96,4,1,96]{1,3,2,0:T(8,128)(2,1)S(1)} %get-tuple-element.3), kind=kLoop, calls=%fused_computation | loop fusion | flops 73728 | bytes 294912 | tf_op jit(solution)/shard_map/stack | solution.py:83
  229.9 4.8 %copy.81 = bf16[96,4,2,96]{3,2,1,0:T(2,128)(2,1)} copy(bf16[96,4,2,96]{1,3,2,0:T(8,128)(2,1)} %pad_maximum_fusion) | data formatting | bytes 294912 | tf_op jit(solution)/shard_map/stack | solution.py:83
  235.8 17.1 %concatenate.27 = bf16[96,768]{1,0:T(8,128)(2,1)} reshape(bf16[48,2,4,2,48,2]{5,4,3,2,1,0:T(8,128)(2,1)} %copy.79) | data formatting | bytes 294912 | tf_op jit(solution)/shard_map/concatenate | solution.py:84
  252.9 1.8 fusion.20
  254.7 1.7 reshape.126
  256.4 5.4 %all-to-all-start.3 = ((bf16[64,4,192]{2,1,0:T(4,128)(2,1)}), bf16[64,4,192]{2,1,0:T(4,128)(2,1)S(1)}, u32[]{:S(2)}, u32[]{:S(2)}) async-start(bf16[64,4,192]{2,1,0:T(4,128)(2,1)} %reshape.126), calls=%async_computation.3 | async-start | bytes 262144 | tf_op jit(solution)/shard_map/all_to_all | solution.py:146
  261.8 1.4 broadcast_multiply_fusion
  263.2 6.5 %all-to-all-done.3 = bf16[64,4,192]{2,1,0:T(4,128)(2,1)S(1)} async-done(((bf16[64,4,192]{2,1,0:T(4,128)(2,1)}), bf16[64,4,192]{2,1,0:T(4,128)(2,1)S(1)}, u32[]{:S(2)}, u32[]{:S(2)}) %all-to-all-start.3) | async-done | bytes 98336 | tf_op jit(solution)/shard_map/all_to_all | solution.py:146
  271.4 1.5 fusion.28
  273.0 1.4 fusion.3
  274.4 5.2 %copy.113 = f32[144,64,128]{2,1,0:T(8,128)} copy(f32[144,64,128]{2,1,0:T(8,128)} %all-reduce.2.cloned.1.call-done) | data formatting | bytes 9437184
  (65 shorter events, 25.5 us)
Async XLA Ops:
  7.2 137.1 %copy-start = (bf16[144,64,128]{2,1,0:T(8,128)(2,1)S(1)}, bf16[144,64,128]{2,1,0:T(8,128)(2,1)}, u32[]{:S(2)}) copy-start(bf16[144,64,128]{2,1,0:T(8,128)(2,1)} %param.11) | copy-start | bytes 7077892
  11.9 1.6 copy-start.4
  11.9 1.9 copy-start.5
  12.0 2.9 %copy-start.6 = (f32[4,2048]{1,0:T(4,128)}, f32[4,2048]{1,0:T(4,128)S(1)}, u32[]{:S(2)}) copy-start(f32[4,2048]{1,0:T(4,128)S(1)} %get-tuple-element.18) | copy-start | bytes 98308
  13.5 1.4 copy-start.1
  13.5 1.4 copy-start.2
  13.5 1.6 copy-start.3
  15.1 11.1 %copy-start.11 = (s32[1,32]{1,0:T(1,128)S(1)}, s32[1,32]{1,0:T(1,128)}, u32[]{:S(2)}) copy-start(s32[1,32]{1,0:T(1,128)} %param.12) | copy-start | bytes 388
  18.4 17.5 %all-to-all-start = ((bf16[4,128,192]{2,0,1:T(4,128)(2,1)}), bf16[4,128,192]{2,0,1:T(4,128)(2,1)}, u32[]{:S(2)}, u32[]{:S(2)}) async-start(bf16[4,128,192]{2,0,1:T(4,128)(2,1)} %copy.65), calls=%async_computation | async-start | bytes 524288 | tf_op jit(solution)/shard_map/all_to_all | solution.py:116
  25.9 248.5 %all-reduce.2.cloned.1.call-start = ((), (), s32[]{:S(2)}) async-start(), calls=%async_computation.4 | async-start | bytes 9437184 | tf_op jit(solution)/shard_map/psum | solution.py:140
  26.6 15.2 %copy-start.8 = (bf16[96,64]{1,0:T(8,128)(2,1)}, bf16[96,64]{1,0:T(8,128)(2,1)S(1)}, u32[]{:S(2)}) copy-start(bf16[96,64]{1,0:T(8,128)(2,1)S(1)} %get-tuple-element.15) | copy-start | bytes 36868
  26.6 15.2 %copy-start.9 = (bf16[96,64]{1,0:T(8,128)(2,1)}, bf16[96,64]{1,0:T(8,128)(2,1)S(1)}, u32[]{:S(2)}) copy-start(bf16[96,64]{1,0:T(8,128)(2,1)S(1)} %get-tuple-element.16) | copy-start | bytes 36868
  149.3 48.4 %all-to-all-start.2 = ((bf16[64,2,2,2,144]{4,3,2,1,0:T(2,128)(2,1)}), bf16[64,2,2,2,144]{4,3,2,1,0:T(2,128)(2,1)}, u32[]{:S(2)}, u32[]{:S(2)}) async-start(bf16[64,2,2,2,144]{4,3,2,1,0:T(2,128)(2,1)} %bitcast.158), calls=%async_computation.2 | async-start | bytes 524288 | tf_op jit(solution)/shard_map/all_to_all | solution.py:141
  254.7 18.3 %copy-start.10 = (bf16[64,64]{1,0:T(8,128)(2,1)S(1)}, bf16[64,64]{1,0:T(8,128)(2,1)}, u32[]{:S(2)}) copy-start(bf16[64,64]{1,0:T(8,128)(2,1)} %param.10) | copy-start | bytes 24580
  256.4 13.3 %all-to-all-start.3 = ((bf16[64,4,192]{2,1,0:T(4,128)(2,1)}), bf16[64,4,192]{2,1,0:T(4,128)(2,1)S(1)}, u32[]{:S(2)}, u32[]{:S(2)}) async-start(bf16[64,4,192]{2,1,0:T(4,128)(2,1)} %reshape.126), calls=%async_computation.3 | async-start | bytes 262144 | tf_op jit(solution)/shard_map/all_to_all | solution.py:146
  271.4 1.6 copy-start.7
Sparse Core Ops, SparseCore 0:
  144.4 120.1 all-reduce.1
